TPU v7x, 256 devices: a whole 4x4x8 slice. The times are simulated.
256 devices in a mesh: row: 16 (over y, x), col: 16 (over z, core).
Axes of the slice: x: 4, y: 4, z: 8, core: 2. Of those that a mesh axis runs over, the one named last changes fastest.
Arguments:
- panel: bfloat16 [15, 32, 512, 512], P(None, 'row', 'col'), may hold values from -0.109375 to 0.109375
- diag_inverse: float32 [6, 32, 512, 512], P(None, 'row', 'col'), as said below
- parents: int32 [5, 32], replicated, may hold values from 0 to 31, as said below
- supernode_sizes: int32 [6, 32], replicated, may hold values from 128 to 512
Outputs:
- cross: float32 [15, 32, 512, 512], P(None, 'row', 'col')
- marginal: float32 [6, 32, 512, 512], P(None, 'row', 'col')
Inputs may be any that keep to these rules, and one draw needn't show every extreme that they name: `parents`: the parent of a supernode g of level d + 1 is a supernode of level d whose index divided by 2 equals g divided by 2, or that minus 1 modulo 32 / 2. `diag_inverse`: every block is symmetric and positive definite.
All inputs are finite; a program needn't handle non-finite values.
Results may differ from a plain program's by a relative error of at most 0.0023.
Values may be sent and summed in bfloat16 or wider, within the bound.
A program may use at most 128 MiB of HBM per device.

v0:
```python
import jax
import jax.numpy as jnp
from jax import lax
from jax.sharding import PartitionSpec as P


def from_behind(x, axis, by):
    size = lax.axis_size(axis)
    return lax.ppermute(x, axis, [(i, (i + by) % size) for i in range(size)])


def turn_over(cross):
    swapped = lax.all_to_all(cross, "col", split_axis=3, concat_axis=2, tiled=True)
    return jnp.swapaxes(swapped, 2, 3)


def shards(panel, diag_inverse, parents, supernode_sizes):
    levels = diag_inverse.shape[0]
    per_row = diag_inverse.shape[1]
    row_count = diag_inverse.shape[2]
    width = diag_inverse.shape[3]
    my_row = lax.axis_index("row")
    my_col = lax.axis_index("col")
    my_nodes = my_row * per_row + jnp.arange(per_row, dtype=jnp.int32)
    my_lines = my_col * row_count + jnp.arange(row_count, dtype=jnp.int32)
    columns = jnp.arange(width, dtype=jnp.int32)
    on_diag = (my_lines[:, None] == columns[None, :]).astype(jnp.float32)
    ancestry_ids = jnp.zeros((0, parents.shape[1]), jnp.int32)
    crosses = []
    diagonals = []
    chain = None
    for level in range(levels):
        own_sizes = supernode_sizes[level][my_nodes]
        live_cols = (columns[None, :] < own_sizes[:, None]).astype(jnp.float32)
        live_lines = (my_lines[None, :] < own_sizes[:, None]).astype(jnp.float32)
        diag_base = (
            diag_inverse[level] * live_lines[:, :, None] * live_cols[:, None, :]
            + on_diag[None] * (1.0 - live_lines)[:, :, None]
        )
        if level == 0:
            diagonal = diag_base
        else:
            parent_ids = parents[level - 1]
            ancestry_ids = jnp.concatenate(
                [ancestry_ids[:, parent_ids], parent_ids[None, :]], axis=0
            )
            my_parents = parent_ids[my_nodes]
            pick_slot = jnp.where(
                my_parents // per_row == my_row,
                my_parents % per_row,
                per_row + my_parents % per_row,
            )
            passed = from_behind(chain, "row", 1)
            ancestry = jnp.take(jnp.concatenate([chain, passed], axis=0), pick_slot, axis=0)
            upper_sizes = supernode_sizes[
                jnp.arange(level, dtype=jnp.int32)[:, None], ancestry_ids[:, my_nodes]
            ]
            live_upper = (my_lines[None, None, :] < upper_sizes[:, :, None]).astype(jnp.float32)
            start = level * (level - 1) // 2
            keep = (live_upper[:, :, :, None] * live_cols[None, :, None, :]).astype(jnp.bfloat16)
            lower = jnp.transpose(panel[start : start + level] * keep, (1, 0, 2, 3))
            whole = lax.all_gather(lower, "col", axis=2, tiled=True).astype(jnp.float32)
            cross = -jnp.einsum(
                "nlmik,nmkj->nlij", ancestry, whole, precision=lax.Precision.HIGHEST
            )
            turned = turn_over(cross)
            diagonal = diag_base - jnp.einsum(
                "nlik,nlkj->nij", turned, whole, precision=lax.Precision.HIGHEST
            )
            crosses.append(jnp.transpose(cross, (1, 0, 2, 3)))
        diagonals.append(diagonal)
        if level < levels - 1:
            if level == 0:
                chain = diagonal[:, None, None]
            else:
                upper = jnp.concatenate([ancestry, cross[:, :, None]], axis=2)
                bottom = jnp.concatenate([turned[:, None], diagonal[:, None, None]], axis=2)
                chain = jnp.concatenate([upper, bottom], axis=1)
    return (jnp.concatenate(crosses, axis=0), jnp.stack(diagonals))


def solution(mesh):
    in_specs = (P(None, "row", "col", None), P(None, "row", "col", None), P(), P())
    out_specs = (P(None, "row", "col", None), P(None, "row", "col", None))
    return jax.shard_map(shards, mesh=mesh, in_specs=in_specs, out_specs=out_specs, check_vma=False)
```

profile of v0, /device:TPU:1, one launch (start us, length us, event | category | flops | bytes accessed | tf_op | source)
XLA Modules:
  0.0 466.2 jit_solution(5601063711213045064)
XLA Ops:
  26.2 2.1 collective-permute-start
  28.4 6.0 %collective-permute-done = f32[2,1,1,32,512]{4,3,0,2,1:T(8,128)S(1)} collective-permute-done((f32[2,1,1,32,512]{4,3,0,2,1:T(8,128)S(1)}, f32[2,1,1,32,512]{4,3,0,2,1:T(8,128)S(1)}, u32[]{:S(2)}, u32[]{:S(2)}) %collective-permute-start) | collective-permute-done | bytes 131104 | tf_op jit(solution)/shard_map/ppermute | solution.py:9
  35.0 23.7 %all-gather.15.cloned.1.call-done = bf16[1,2,512,512]{3,2,1,0:T(8,128)(2,1)} async-done(((bf16[1,2,32,512]{3,2,1,0:T(8,128)(2,1)}), bf16[1,2,512,512]{3,2,1,0:T(8,128)(2,1)}) %all-gather.15.cloned.1.call-update) | async-done | bytes 1048592 | tf_op jit(solution)/shard_map/all_gather | solution.py:62
  58.7 2.6 bitcast_dynamic-update-slice_fusion.4
  62.7 4.7 all-to-all-start
  68.8 7.5 %all-to-all-done = f32[16,1,2048]{2,1,0:T(1,128)S(1)} async-done(((f32[16,1,2048]{2,1,0:T(1,128)}), f32[16,1,2048]{2,1,0:T(1,128)S(1)}, u32[]{:S(2)}, u32[]{:S(2)}) %all-to-all-start) | async-done | bytes 131104 | tf_op jit(solution)/shard_map/all_to_all | solution.py:13
  81.4 15.8 %collective-permute-done.1 = f32[2,2,2,32,512]{4,3,0,2,1:T(8,128)S(1)} collective-permute-done((f32[2,2,2,32,512]{4,3,0,2,1:T(8,128)S(1)}, f32[2,2,2,32,512]{4,3,0,2,1:T(8,128)S(1)}, u32[]{:S(2)}, u32[]{:S(2)}) %collective-permute-start.1) | collective-permute-done | bytes 524320 | tf_op jit(solution)/shard_map/ppermute | solution.py:9
  99.0 3.5 bitcast_dynamic-update-slice_fusion.3
  105.0 4.5 all-to-all-start.1
  112.4 11.4 %all-to-all-done.1 = f32[16,1,4096]{2,1,0:T(1,128)S(1)} async-done(((f32[16,1,4096]{2,1,0:T(1,128)}), f32[16,1,4096]{2,1,0:T(1,128)S(1)}, u32[]{:S(2)}, u32[]{:S(2)}) %all-to-all-start.1) | async-done | bytes 262176 | tf_op jit(solution)/shard_map/all_to_all | solution.py:13
  126.9 2.9 copy.212
  131.4 2.7 bitcast_dynamic-update-slice_fusion.7
  138.1 27.5 %collective-permute-done.2 = f32[2,3,3,32,512]{4,3,2,1,0:T(8,128)} collective-permute-done((f32[2,3,3,32,512]{4,3,2,1,0:T(8,128)S(1)}, f32[2,3,3,32,512]{4,3,2,1,0:T(8,128)}, u32[]{:S(2)}, u32[]{:S(2)}) %collective-permute-start.2) | collective-permute-done | bytes 1179680 | tf_op jit(solution)/shard_map/ppermute | solution.py:9
  165.6 3.0 pad_maximum_fusion.2
  168.6 2.3 gather_fusion.12
  171.2 4.3 bitcast_dynamic-update-slice_fusion.2
  176.6 2.3 reshape.1603
  178.9 18.5 %all_to_all.90 = f32[16,1,6144]{2,1,0:T(1,128)S(1)} all-to-all(f32[16,1,6144]{2,1,0:T(1,128)} %reshape.1603), channel_id=1, replica_groups=mesh['row'=16,'col'=16] {'col'}, dimensions={0} | all-to-all | bytes 786432 | tf_op jit(solution)/shard_map/all_to_all | solution.py:13
  197.4 2.4 reduce.8
  199.8 2.3 reshape.1604
  202.1 2.1 copy.211
  206.2 4.1 bitcast_dynamic-update-slice_fusion.6
  212.6 50.1 %collective-permute-done.3 = f32[2,4,4,32,512]{4,3,2,1,0:T(8,128)} collective-permute-done((f32[2,4,4,32,512]{4,3,2,1,0:T(8,128)}, f32[2,4,4,32,512]{4,3,2,1,0:T(8,128)}, u32[]{:S(2)}, u32[]{:S(2)}) %collective-permute-start.3) | collective-permute-done | bytes 2097184 | tf_op jit(solution)/shard_map/ppermute | solution.py:9
  262.7 4.2 pad_maximum_fusion.1
  266.9 4.2 gather_fusion.18
  273.1 4.8 %bitcast_dynamic-update-slice_fusion.1 = (f32[15,2,32,512]{3,2,0,1:T(8,128)}, f32[2,4,32,512]{3,2,1,0:T(8,128)S(1)}) fusion(f32[15,2,32,512]{3,2,0,1:T(8,128)} %get-tuple-element.48, f32[2,4,4,32,512]{4,3,2,1,0:T(8,128)S(1)} %broadcast_select_fusion, bf16[2,4,512,512]{3,2,1,0:T(8,128)(2,1)} %all-gather.11.cloned.1.call-done), kind=kOutput, calls=%fused_computation.81 | convolution fusion | flops 3221356544 | bytes 7340032 | tf_op jit(solution)/shard_map/nlmik,nmkj->nlij/dot_general | solution.py:63
  279.7 2.8 reshape.1605
  282.6 21.0 %all_to_all.91 = f32[16,1,8192]{2,1,0:T(1,128)} all-to-all(f32[16,1,8192]{2,1,0:T(1,128)S(1)} %reshape.1605), channel_id=1, replica_groups=mesh['row'=16,'col'=16] {'col'}, dimensions={0} | all-to-all | bytes 1048576 | tf_op jit(solution)/shard_map/all_to_all | solution.py:13
  303.6 2.9 reduce.9
  306.5 2.5 reshape.1606
  309.0 4.1 copy.210
  313.1 2.3 all_to_all.80
  315.4 4.9 %bitcast_dynamic-update-slice_fusion.5 = (f32[6,2,32,512]{3,2,1,0:T(8,128)}, f32[2,32,512]{2,1,0:T(8,128)S(1)}) fusion(f32[6,2,32,512]{3,2,1,0:T(8,128)} %get-tuple-element.58, bf16[2,4,512,512]{3,2,1,0:T(8,128)(2,1)} %all-gather.11.cloned.1.call-done, f32[2,4,512,32]{2,3,1,0:T(8,128)S(1)} %all_to_all.80, f32[2,32]{1,0:T(2,128)S(1)} %get-tuple-element.39, ...), kind=kOutput, calls=%fused_computation.105 | convolution fusion | flops 805470208 | bytes 5181952 | tf_op jit(solution)/shard_map/nlik,nlkj->nij/dot_general | solution.py:67
  320.4 2.1 maximum_maximum_fusion
  323.4 74.8 %collective-permute-done.4 = f32[2,5,5,32,512]{4,3,2,1,0:T(8,128)} collective-permute-done((f32[2,5,5,32,512]{4,3,2,1,0:T(8,128)}, f32[2,5,5,32,512]{4,3,2,1,0:T(8,128)}, u32[]{:S(2)}, u32[]{:S(2)}) %collective-permute-start.4) | collective-permute-done | bytes 3276832 | tf_op jit(solution)/shard_map/ppermute | solution.py:9
  398.2 4.7 %pad_maximum_fusion = f32[4,5,5,32,512]{4,3,2,1,0:T(8,128)} fusion(f32[2,5,5,32,512]{4,3,2,1,0:T(8,128)} %collective-permute-done.4, f32[2,1,1,32,512]{4,3,2,1,0:T(8,128)S(1)} %bitcast.445, f32[2,1,4,32,512]{4,3,2,1,0:T(8,128)S(1)} %bitcast.421, f32[2,4,1,32,512]{4,3,2,1,0:T(8,128)S(1)} %bitcast.436, f32[2,4,4,32,512]{4,3,2,1,0:T(8,128)S(1)} %broadcast_select_fusion), kind=kLoop, calls=%fused_computation.30 | loop fusion | flops 6553600 | bytes 13107200 | tf_op jit(solution)/shard_map/concatenate | solution.py:54
  402.9 3.6 gather_fusion.24
  406.6 6.4 %bitcast_dynamic-update-slice_fusion = (f32[15,2,32,512]{3,2,0,1:T(8,128)}, f32[2,5,32,512]{3,2,1,0:T(8,128)}) fusion(f32[15,2,32,512]{3,2,0,1:T(8,128)} %get-tuple-element.50, bf16[2,5,512,512]{3,2,1,0:T(8,128)(2,1)} %all-gather.13.cloned.1.call-done, f32[2,5,5,32,512]{4,3,2,1,0:T(8,128)S(1)} %gather_fusion.24, pred[2]{0:T(512)(128)(4,1)S(1)} %compare_and_fusion), kind=kOutput, calls=%fused_computation.76 | convolution fusion | flops 5034147840 | bytes 9830402 | tf_op jit(solution)/shard_map/nlmik,nmkj->nlij/dot_general | solution.py:63
  412.9 3.1 copy.173
  416.0 3.4 reshape.1607
  419.4 4.3 all-to-all-start.4
  423.7 3.1 copy.175
  426.8 16.8 %all-to-all-done.4 = f32[16,1,10240]{2,1,0:T(1,128)S(1)} async-done(((f32[16,1,10240]{2,1,0:T(1,128)}), f32[16,1,10240]{2,1,0:T(1,128)S(1)}, u32[]{:S(2)}, u32[]{:S(2)}) %all-to-all-start.4) | async-done | bytes 655392 | tf_op jit(solution)/shard_map/all_to_all | solution.py:13
  443.5 2.2 reduce.10
  445.7 2.2 reshape.1608
  447.9 3.1 copy.209
  451.0 2.5 all_to_all.84
  453.5 5.7 %fusion.43 = f32[6,2,32,512]{3,2,1,0:T(8,128)} fusion(f32[6,2,32,512]{3,2,1,0:T(8,128)} %get-tuple-element.60, bf16[2,5,512,512]{3,2,1,0:T(8,128)(2,1)} %all-gather.13.cloned.1.call-done, f32[2,5,512,32]{2,3,1,0:T(8,128)S(1)} %all_to_all.84, f32[6,2,32,512]{3,2,1,0:T(8,128)} %param.5, f32[2,32]{1,0:T(2,128)S(1)} %get-tuple-element.38, ...), kind=kOutput, calls=%fused_computation.67 | convolution fusion | flops 1006796800 | bytes 6230528 | tf_op jit(solution)/shard_map/nlik,nlkj->nij/dot_general | solution.py:67
  (155 shorter events, 53.7 us)
Async XLA Ops:
  7.2 8.7 %copy-start.5 = (s32[5,32]{1,0:T(8,128)S(1)}, s32[5,32]{1,0:T(8,128)}, u32[]{:S(2)}) copy-start(s32[5,32]{1,0:T(8,128)} %param.6) | copy-start | bytes 1924
  7.2 7.9 %copy-start.4 = (bf16[15,2,32,512]{3,2,1,0:T(8,128)(2,1)S(1)}, bf16[15,2,32,512]{3,2,1,0:T(8,128)(2,1)}, u32[]{:S(2)}) copy-start(bf16[15,2,32,512]{3,2,1,0:T(8,128)(2,1)} %param.4) | copy-start | bytes 2949124
  7.2 51.5 %all-gather.15.cloned.1.call-start = ((), (), s32[]{:S(2)}) async-start(), calls=%async_computation.9 | async-start | bytes 1114112 | tf_op jit(solution)/shard_map/all_gather | solution.py:62
  8.8 8.6 %copy-start = (s32[6,32]{1,0:T(8,128)S(1)}, s32[6,32]{1,0:T(8,128)}, u32[]{:S(2)}) copy-start(s32[6,32]{1,0:T(8,128)} %param.7) | copy-start | bytes 2308
  15.8 83.2 %all-gather.7.cloned.1.call-start = ((), (), s32[]{:S(2)}) async-start(), calls=%async_computation.5 | async-start | bytes 2228224 | tf_op jit(solution)/shard_map/all_gather | solution.py:62
  19.2 152.0 %all-gather.9.cloned.1.call-start = ((), (), s32[]{:S(2)}) async-start(), calls=%async_computation.6 | async-start | bytes 3342336 | tf_op jit(solution)/shard_map/all_gather | solution.py:62
  21.3 4.8 %copy-start.3 = (f32[6,2,32,512]{3,2,1,0:T(8,128)S(1)}, f32[6,2,32,512]{3,2,1,0:T(8,128)}, u32[]{:S(2)}) copy-start(f32[6,2,32,512]{3,2,1,0:T(8,128)} %param.5) | copy-start | bytes 2359300
  22.5 250.6 %all-gather.11.cloned.1.call-start = ((), (), s32[]{:S(2)}) async-start(), calls=%async_computation.7 | async-start | bytes 4456448 | tf_op jit(solution)/shard_map/all_gather | solution.py:62
  26.2 8.2 %collective-permute-start = (f32[2,1,1,32,512]{4,3,0,2,1:T(8,128)S(1)}, f32[2,1,1,32,512]{4,3,0,2,1:T(8,128)S(1)}, u32[]{:S(2)}, u32[]{:S(2)}) collective-permute-start(f32[2,1,1,32,512]{4,3,0,2,1:T(8,128)S(1)} %fusion.71), channel_id=1, source_target_pairs={{0,16},{16,32},{32,48},{48,64},{64,80},{80,96},{96,112},{112,128},... | collective-permute-start | bytes 393224 | tf_op jit(solution)/shard_map/ppermute | solution.py:9
  61.5 17.3 %copy-start.2 = (bf16[1,2,512,512]{3,2,1,0:T(8,128)(2,1)S(1)}, bf16[1,2,512,512]{3,2,1,0:T(8,128)(2,1)}, u32[]{:S(2)}) copy-start(bf16[1,2,512,512]{3,2,1,0:T(8,128)(2,1)} %all-gather.15.cloned.1.call-done) | copy-start | bytes 3145732
  62.7 13.6 %all-to-all-start = ((f32[16,1,2048]{2,1,0:T(1,128)}), f32[16,1,2048]{2,1,0:T(1,128)S(1)}, u32[]{:S(2)}, u32[]{:S(2)}) async-start(f32[16,1,2048]{2,1,0:T(1,128)} %reshape.1599), calls=%async_computation | async-start | bytes 262144 | tf_op jit(solution)/shard_map/all_to_all | solution.py:13
  80.1 17.1 %collective-permute-start.1 = (f32[2,2,2,32,512]{4,3,0,2,1:T(8,128)S(1)}, f32[2,2,2,32,512]{4,3,0,2,1:T(8,128)S(1)}, u32[]{:S(2)}, u32[]{:S(2)}) collective-permute-start(f32[2,2,2,32,512]{4,3,0,2,1:T(8,128)S(1)} %maximum_maximum_fusion.3), channel_id=1, source_target_pairs={{0,16},{16,32},{32,48},{48,64},{64,80},{80,96},{96,112},{112,128},... | collective-permute-start | bytes 1572872 | tf_op jit(solution)/shard_map/ppermute | solution.py:9
  105.0 18.8 %all-to-all-start.1 = ((f32[16,1,4096]{2,1,0:T(1,128)}), f32[16,1,4096]{2,1,0:T(1,128)S(1)}, u32[]{:S(2)}, u32[]{:S(2)}) async-start(f32[16,1,4096]{2,1,0:T(1,128)} %reshape.1601), calls=%async_computation.1 | async-start | bytes 524288 | tf_op jit(solution)/shard_map/all_to_all | solution.py:13
  109.5 297.0 %all-gather.13.cloned.1.call-start = ((), (), s32[]{:S(2)}) async-start(), calls=%async_computation.8 | async-start | bytes 5570560 | tf_op jit(solution)/shard_map/all_gather | solution.py:62
  125.0 6.4 %copy-start.1 = (bf16[2,2,512,512]{3,2,1,0:T(8,128)(2,1)S(1)}, bf16[2,2,512,512]{3,2,1,0:T(8,128)(2,1)}, u32[]{:S(2)}) copy-start(bf16[2,2,512,512]{3,2,1,0:T(8,128)(2,1)} %all-gather.7.cloned.1.call-done) | copy-start | bytes 6291460
  134.2 31.4 %collective-permute-start.2 = (f32[2,3,3,32,512]{4,3,2,1,0:T(8,128)S(1)}, f32[2,3,3,32,512]{4,3,2,1,0:T(8,128)}, u32[]{:S(2)}, u32[]{:S(2)}) collective-permute-start(f32[2,3,3,32,512]{4,3,2,1,0:T(8,128)S(1)} %maximum_maximum_fusion.2), channel_id=1, source_target_pairs={{0,16},{16,32},{32,48},{48,64},{64,80},{80,96},{96,112},{112,128},... | collective-permute-start | bytes 3538952 | tf_op jit(solution)/shard_map/ppermute | solution.py:9
  211.9 50.8 %collective-permute-start.3 = (f32[2,4,4,32,512]{4,3,2,1,0:T(8,128)}, f32[2,4,4,32,512]{4,3,2,1,0:T(8,128)}, u32[]{:S(2)}, u32[]{:S(2)}) collective-permute-start(f32[2,4,4,32,512]{4,3,2,1,0:T(8,128)} %maximum_maximum_fusion.1), channel_id=1, source_target_pairs={{0,16},{16,32},{32,48},{48,64},{64,80},{80,96},{96,112},{112,128},... | collective-permute-start | bytes 6291464 | tf_op jit(solution)/shard_map/ppermute | solution.py:9
  322.5 75.7 %collective-permute-start.4 = (f32[2,5,5,32,512]{4,3,2,1,0:T(8,128)}, f32[2,5,5,32,512]{4,3,2,1,0:T(8,128)}, u32[]{:S(2)}, u32[]{:S(2)}) collective-permute-start(f32[2,5,5,32,512]{4,3,2,1,0:T(8,128)} %maximum_maximum_fusion), channel_id=1, source_target_pairs={{0,16},{16,32},{32,48},{48,64},{64,80},{80,96},{96,112},{112,128},... | collective-permute-start | bytes 9830408 | tf_op jit(solution)/shard_map/ppermute | solution.py:9
  419.4 24.2 %all-to-all-start.4 = ((f32[16,1,10240]{2,1,0:T(1,128)}), f32[16,1,10240]{2,1,0:T(1,128)S(1)}, u32[]{:S(2)}, u32[]{:S(2)}) async-start(f32[16,1,10240]{2,1,0:T(1,128)} %reshape.1607), calls=%async_computation.4 | async-start | bytes 1310720 | tf_op jit(solution)/shard_map/all_to_all | solution.py:13
Sparse Core Ops, SparseCore 0:
  15.9 42.7 all-gather.14
  60.5 38.4 all-gather.6
  100.9 42.6 all-gather.8
  145.3 41.1 all-gather.10
  188.2 47.1 all-gather.12
where the time goes:
time: 474 us; the launch traced here: 466 us
  waiting for transfers between devices  235 us (50%)
  local copies, waits for them, and re-layouts  82.8 us (17%)
  matrix products  40.3 us (9%)
  blocking collectives  39.5 us (8%)
  other arithmetic  35.3 us (7%)
  starting transfers between devices  19.1 us (4%)
  between operations  14.7 us (3%)
    ppermute x5, waiting for transfers between devices, from_behind(): return lax.ppermute(x, axis, [(i, (i + by) % size) for i in range(size)])  174 us
    all_to_all x2, blocking collectives, turn_over(): lax.all_to_all(cross, 'col', split_axis=3, concat_axis=2, tiled=True)  39.5 us
    all_to_all x3, waiting for transfers between devices, turn_over(): lax.all_to_all(cross, 'col', split_axis=3, concat_axis=2, tiled=True)  35.6 us
    all_gather x5, waiting for transfers between devices, shards(): whole = lax.all_gather(lower, 'col', axis=2, tiled=True).astype(jnp.float32)  24.7 us
    unnamed x26, local copies, waits for them, and re-layouts  24.1 us
    all_to_all x11, local copies, waits for them, and re-layouts, turn_over(): lax.all_to_all(cross, 'col', split_axis=3, concat_axis=2, tiled=True)  21.7 us
    dot_general x5, matrix products, shards(): jnp.einsum('nlmik,nmkj->nlij', ancestry, whole, precision=lax.Precision.H...  21.6 us
    dot_general x5, matrix products, shards(): jnp.einsum('nlik,nlkj->nij', turned, whole, precision=lax.Precision.HIGHEST)  18.7 us
  transfers between devices with their start and end apart: 13, of which 10 were waited for; matrix products, arithmetic and copies ran while one was open for 25% of the time, Pallas kernels for 0%

commit v1 on v0

--- a/solution.py
+++ b/solution.py
@@ -59,7 +59,9 @@
             start = level * (level - 1) // 2
             keep = (live_upper[:, :, :, None] * live_cols[None, :, None, :]).astype(jnp.bfloat16)
             lower = jnp.transpose(panel[start : start + level] * keep, (1, 0, 2, 3))
-            whole = lax.all_gather(lower, "col", axis=2, tiled=True).astype(jnp.float32)
+            whole = jnp.concatenate(
+                lax.all_to_all(jnp.stack([lower] * lax.axis_size("col")), "col", 0, 0), axis=2
+            ).astype(jnp.float32)
             cross = -jnp.einsum(
                 "nlmik,nmkj->nlij", ancestry, whole, precision=lax.Precision.HIGHEST
             )

time: 474 us -> 602 us (1.27)
  waiting for transfers between devices: 235 us -> 340 us
  starting transfers between devices: 19.1 us -> 60.1 us
  blocking collectives: 39.5 us -> 0 us
  local copies, waits for them, and re-layouts: 82.8 us -> 119 us
  between operations: 14.7 us -> 1.38 us
  matrix products: 40.3 us -> 33.8 us
    all_to_all x0 -> x5, waiting for transfers between devices: none -> 230 us  [shards(): lax.all_to_all(jnp.stack([lower] * lax.axis_size('col')), 'col', 0, 0)]
    ppermute x5, waiting for transfers between devices: 174 us -> 48.6 us  [from_behind(): return lax.ppermute(x, axis, [(i, (i + by) % size) for i in range(size)])]
    all_to_all x2 -> x0, blocking collectives: 39.5 us -> none  [turn_over(): lax.all_to_all(cross, 'col', split_axis=3, concat_axis=2, tiled=True)]
    all_to_all x0 -> x5, starting transfers between devices: none -> 28.3 us  [shards(): lax.all_to_all(jnp.stack([lower] * lax.axis_size('col')), 'col', 0, 0)]
    all_to_all x3 -> x5, waiting for transfers between devices: 35.6 us -> 60.8 us  [turn_over(): lax.all_to_all(cross, 'col', split_axis=3, concat_axis=2, tiled=True)]
    all_gather x5 -> x0, waiting for transfers between devices: 24.7 us -> none  [shards(): whole = lax.all_gather(lower, 'col', axis=2, tiled=True).astype(jnp.float32)]
    reshape x0 -> x5, local copies, waits for them, and re-layouts: none -> 14.7 us  [shards(): jnp.concatenate(lax.all_to_all(jnp.stack([lower] * lax.axis_size('col')),...]
    all_to_all x3 -> x5, starting transfers between devices: 13.5 us -> 25 us  [turn_over(): lax.all_to_all(cross, 'col', split_axis=3, concat_axis=2, tiled=True)]
  transfers between devices with their start and end apart: 13 -> 15, of which waited for: 10 -> 13; matrix products, arithmetic and copies ran while one was open for 25% -> 14% of each run, Pallas kernels for 0% -> 0%
where the time goes in v1:
time: 602 us; the launch traced here: 593 us
  waiting for transfers between devices  340 us (56%)
  local copies, waits for them, and re-layouts  119 us (20%)
  starting transfers between devices  60.1 us (10%)
  other arithmetic  39.3 us (7%)
  matrix products  33.8 us (6%)
    all_to_all x5, waiting for transfers between devices, shards(): lax.all_to_all(jnp.stack([lower] * lax.axis_size('col')), 'col', 0, 0)  230 us
    all_to_all x5, waiting for transfers between devices, turn_over(): lax.all_to_all(cross, 'col', split_axis=3, concat_axis=2, tiled=True)  60.8 us
    ppermute x5, waiting for transfers between devices, from_behind(): return lax.ppermute(x, axis, [(i, (i + by) % size) for i in range(size)])  48.6 us
    unnamed x54, local copies, waits for them, and re-layouts  30.4 us
    all_to_all x5, starting transfers between devices, shards(): lax.all_to_all(jnp.stack([lower] * lax.axis_size('col')), 'col', 0, 0)  28.3 us
    all_to_all x5, starting transfers between devices, turn_over(): lax.all_to_all(cross, 'col', split_axis=3, concat_axis=2, tiled=True)  25 us
    all_to_all x11, local copies, waits for them, and re-layouts, turn_over(): lax.all_to_all(cross, 'col', split_axis=3, concat_axis=2, tiled=True)  23.7 us
    dot_general x5, matrix products, shards(): jnp.einsum('nlik,nlkj->nij', turned, whole, precision=lax.Precision.HIGHEST)  18 us
  transfers between devices with their start and end apart: 15, of which 13 were waited for; matrix products, arithmetic and copies ran while one was open for 14% of the time, Pallas kernels for 0%

profile of v1, /device:TPU:1, one launch (start us, length us, event | category | flops | bytes accessed | tf_op | source)
XLA Modules:
  0.0 593.3 jit_solution(4759252900282844543)
XLA Ops:
  10.1 10.0 %all-to-all-start = ((bf16[16,2,1,32,512]{4,3,1,2,0:T(8,128)(2,1)}), bf16[16,2,1,32,512]{4,3,1,2,0:T(8,128)(2,1)S(1)}, u32[]{:S(2)}, u32[]{:S(2)}) async-start(bf16[16,2,1,32,512]{4,3,1,2,0:T(8,128)(2,1)} %stack.22), calls=%async_computation | async-start | bytes 2097152 | tf_op jit(solution)/shard_map/all_to_all | solution.py:63
  25.2 4.4 collective-permute-done
  30.2 17.9 %all-to-all-done = bf16[16,2,1,32,512]{4,3,1,2,0:T(8,128)(2,1)S(1)} async-done(((bf16[16,2,1,32,512]{4,3,1,2,0:T(8,128)(2,1)}), bf16[16,2,1,32,512]{4,3,1,2,0:T(8,128)(2,1)S(1)}, u32[]{:S(2)}, u32[]{:S(2)}) %all-to-all-start) | async-done | bytes 1048608 | tf_op jit(solution)/shard_map/all_to_all | solution.py:63
  50.9 3.4 all-to-all-start.1
  55.5 7.8 %all-to-all-done.1 = f32[16,1,2048]{2,1,0:T(1,128)S(1)} async-done(((f32[16,1,2048]{2,1,0:T(1,128)}), f32[16,1,2048]{2,1,0:T(1,128)S(1)}, u32[]{:S(2)}, u32[]{:S(2)}) %all-to-all-start.1) | async-done | bytes 131104 | tf_op jit(solution)/shard_map/all_to_all | solution.py:13
  64.8 4.3 all-to-all-start.2
  77.2 15.9 %collective-permute-done.1 = f32[2,2,2,32,512]{4,3,0,2,1:T(8,128)S(1)} collective-permute-done((f32[2,2,2,32,512]{4,3,0,2,1:T(8,128)S(1)}, f32[2,2,2,32,512]{4,3,0,2,1:T(8,128)S(1)}, u32[]{:S(2)}, u32[]{:S(2)}) %collective-permute-start.1) | collective-permute-done | bytes 524320 | tf_op jit(solution)/shard_map/ppermute | solution.py:9
  94.0 24.1 %all-to-all-done.2 = bf16[16,2,2,32,512]{4,3,2,1,0:T(8,128)(2,1)} async-done(((bf16[16,2,2,32,512]{4,3,2,1,0:T(8,128)(2,1)}), bf16[16,2,2,32,512]{4,3,2,1,0:T(8,128)(2,1)}, u32[]{:S(2)}, u32[]{:S(2)}) %all-to-all-start.2) | async-done | bytes 2097184 | tf_op jit(solution)/shard_map/all_to_all | solution.py:63
  122.9 3.0 reshape.1650
  126.0 4.8 all-to-all-start.3
  132.9 9.5 %all-to-all-done.3 = f32[16,1,4096]{2,1,0:T(1,128)S(1)} async-done(((f32[16,1,4096]{2,1,0:T(1,128)}), f32[16,1,4096]{2,1,0:T(1,128)S(1)}, u32[]{:S(2)}, u32[]{:S(2)}) %all-to-all-start.3) | async-done | bytes 262176 | tf_op jit(solution)/shard_map/all_to_all | solution.py:13
  144.5 4.6 all-to-all-start.4
  162.7 28.3 %collective-permute-done.2 = f32[2,3,3,32,512]{4,3,2,1,0:T(8,128)} collective-permute-done((f32[2,3,3,32,512]{4,3,2,1,0:T(8,128)S(1)}, f32[2,3,3,32,512]{4,3,2,1,0:T(8,128)}, u32[]{:S(2)}, u32[]{:S(2)}) %collective-permute-start.2) | collective-permute-done | bytes 1179680 | tf_op jit(solution)/shard_map/ppermute | solution.py:9
  191.0 3.1 pad_maximum_fusion.2
  197.7 21.9 %all-to-all-done.4 = bf16[16,2,3,32,512]{4,3,2,1,0:T(8,128)(2,1)} async-done(((bf16[16,2,3,32,512]{4,3,2,1,0:T(8,128)(2,1)}), bf16[16,2,3,32,512]{4,3,2,1,0:T(8,128)(2,1)}, u32[]{:S(2)}, u32[]{:S(2)}) %all-to-all-start.4) | async-done | bytes 3145760 | tf_op jit(solution)/shard_map/all_to_all | solution.py:63
  224.3 3.1 copy.155
  227.4 3.7 reshape.1652
  231.2 5.5 all-to-all-start.5
  238.8 12.4 %all-to-all-done.5 = f32[16,1,6144]{2,1,0:T(1,128)} async-done(((f32[16,1,6144]{2,1,0:T(1,128)}), f32[16,1,6144]{2,1,0:T(1,128)}, u32[]{:S(2)}, u32[]{:S(2)}) %all-to-all-start.5) | async-done | bytes 393248 | tf_op jit(solution)/shard_map/all_to_all | solution.py:13
  253.8 4.7 all-to-all-start.6
  258.4 3.4 reduce.8
  261.8 3.5 reshape.1653
  265.3 3.5 copy.198
  271.6 3.4 bitcast_dynamic-update-slice_fusion.6
  277.9 73.1 %all-to-all-done.6 = bf16[16,2,4,32,512]{4,3,2,1,0:T(8,128)(2,1)} async-done(((bf16[16,2,4,32,512]{4,3,2,1,0:T(8,128)(2,1)}), bf16[16,2,4,32,512]{4,3,2,1,0:T(8,128)(2,1)}, u32[]{:S(2)}, u32[]{:S(2)}) %all-to-all-start.6) | async-done | bytes 4194336 | tf_op jit(solution)/shard_map/all_to_all | solution.py:63
  351.0 5.0 copy.160
  356.0 4.2 pad_maximum_fusion.1
  360.2 4.2 gather_fusion.18
  371.7 3.5 reshape.1654
  375.2 5.5 all-to-all-start.7
  383.6 14.3 %all-to-all-done.7 = f32[16,1,8192]{2,1,0:T(1,128)S(1)} async-done(((f32[16,1,8192]{2,1,0:T(1,128)}), f32[16,1,8192]{2,1,0:T(1,128)S(1)}, u32[]{:S(2)}, u32[]{:S(2)}) %all-to-all-start.7) | async-done | bytes 524320 | tf_op jit(solution)/shard_map/all_to_all | solution.py:13
  397.9 3.0 stack.26
  401.0 4.7 all-to-all-start.8
  411.1 4.2 copy.197
  417.6 4.9 bitcast_dynamic-update-slice_fusion.5
  427.1 93.3 %all-to-all-done.8 = bf16[16,2,5,32,512]{4,3,2,1,0:T(8,128)(2,1)} async-done(((bf16[16,2,5,32,512]{4,3,2,1,0:T(8,128)(2,1)}), bf16[16,2,5,32,512]{4,3,2,1,0:T(8,128)(2,1)}, u32[]{:S(2)}, u32[]{:S(2)}) %all-to-all-start.8) | async-done | bytes 5242912 | tf_op jit(solution)/shard_map/all_to_all | solution.py:63
  520.4 5.7 copy.166
  526.0 4.7 pad_maximum_fusion
  530.7 5.3 gather_fusion.24
  536.0 7.3 %bitcast_dynamic-update-slice_fusion = (f32[15,2,32,512]{3,2,0,1:T(8,128)}, f32[2,5,32,512]{3,2,1,0:T(8,128)}) fusion(f32[15,2,32,512]{3,2,0,1:T(8,128)} %get-tuple-element.50, bf16[2,5,512,512,1]{3,2,1,4,0:T(8,128)(2,1)} %bitcast.403, f32[2,5,5,32,512]{4,3,2,1,0:T(8,128)} %gather_fusion.24, pred[2]{0:T(512)(128)(4,1)S(1)} %compare_and_fusion), kind=kOutput, calls=%fused_computation.67 | convolution fusion | flops 5034147840 | bytes 9830402 | tf_op jit(solution)/shard_map/nlmik,nmkj->nlij/dot_general | solution.py:65
  543.4 3.1 copy.168
  546.4 3.4 reshape.1656
  549.8 5.8 all-to-all-start.9
  555.6 3.1 copy.170
  558.7 16.8 %all-to-all-done.9 = f32[16,1,10240]{2,1,0:T(1,128)S(1)} async-done(((f32[16,1,10240]{2,1,0:T(1,128)}), f32[16,1,10240]{2,1,0:T(1,128)S(1)}, u32[]{:S(2)}, u32[]{:S(2)}) %all-to-all-start.9) | async-done | bytes 655392 | tf_op jit(solution)/shard_map/all_to_all | solution.py:13
  575.4 3.2 reduce.10
  578.6 3.3 reshape.1657
  587.4 5.7 fusion.17
  (190 shorter events, 98.6 us)
Async XLA Ops:
  0.6 6.1 %copy-start = (s32[6,32]{1,0:T(8,128)S(1)}, s32[6,32]{1,0:T(8,128)}, u32[]{:S(2)}) copy-start(s32[6,32]{1,0:T(8,128)} %param.7) | copy-start | bytes 2308
  0.6 4.9 copy-start.16
  1.6 379.2 %copy-start.11 = (s32[1024]{0:T(1024)}, s32[1024]{0:T(1024)S(1)}, u32[]{:S(2)}) copy-start(s32[1024]{0:T(1024)S(1)} %pad_clamp_fusion.9) | copy-start | bytes 12292
  5.5 15.4 %copy-start.10 = (f32[6,2,32,512]{3,2,1,0:T(8,128)S(1)}, f32[6,2,32,512]{3,2,1,0:T(8,128)}, u32[]{:S(2)}) copy-start(f32[6,2,32,512]{3,2,1,0:T(8,128)} %param.5) | copy-start | bytes 2359300
  10.1 38.0 %all-to-all-start = ((bf16[16,2,1,32,512]{4,3,1,2,0:T(8,128)(2,1)}), bf16[16,2,1,32,512]{4,3,1,2,0:T(8,128)(2,1)S(1)}, u32[]{:S(2)}, u32[]{:S(2)}) async-start(bf16[16,2,1,32,512]{4,3,1,2,0:T(8,128)(2,1)} %stack.22), calls=%async_computation | async-start | bytes 2097152 | tf_op jit(solution)/shard_map/all_to_all | solution.py:63
  20.9 8.6 %collective-permute-start = (f32[2,1,1,32,512]{4,3,0,2,1:T(8,128)S(1)}, f32[2,1,1,32,512]{4,3,0,2,1:T(8,128)S(1)}, u32[]{:S(2)}, u32[]{:S(2)}) collective-permute-start(f32[2,1,1,32,512]{4,3,0,2,1:T(8,128)S(1)} %fusion.43), channel_id=1, source_target_pairs={{0,16},{16,32},{32,48},{48,64},{64,80},{80,96},{96,112},{112,128},... | collective-permute-start | bytes 393224 | tf_op jit(solution)/shard_map/ppermute | solution.py:9
  50.9 12.3 %all-to-all-start.1 = ((f32[16,1,2048]{2,1,0:T(1,128)}), f32[16,1,2048]{2,1,0:T(1,128)S(1)}, u32[]{:S(2)}, u32[]{:S(2)}) async-start(f32[16,1,2048]{2,1,0:T(1,128)} %reshape.1648), calls=%async_computation.1 | async-start | bytes 262144 | tf_op jit(solution)/shard_map/all_to_all | solution.py:13
  64.8 53.2 %all-to-all-start.2 = ((bf16[16,2,2,32,512]{4,3,2,1,0:T(8,128)(2,1)}), bf16[16,2,2,32,512]{4,3,2,1,0:T(8,128)(2,1)}, u32[]{:S(2)}, u32[]{:S(2)}) async-start(bf16[16,2,2,32,512]{4,3,2,1,0:T(8,128)(2,1)} %stack.23), calls=%async_computation.2 | async-start | bytes 4194304 | tf_op jit(solution)/shard_map/all_to_all | solution.py:63
  75.9 17.3 %collective-permute-start.1 = (f32[2,2,2,32,512]{4,3,0,2,1:T(8,128)S(1)}, f32[2,2,2,32,512]{4,3,0,2,1:T(8,128)S(1)}, u32[]{:S(2)}, u32[]{:S(2)}) collective-permute-start(f32[2,2,2,32,512]{4,3,0,2,1:T(8,128)S(1)} %maximum_maximum_fusion.3), channel_id=1, source_target_pairs={{0,16},{16,32},{32,48},{48,64},{64,80},{80,96},{96,112},{112,128},... | collective-permute-start | bytes 1572872 | tf_op jit(solution)/shard_map/ppermute | solution.py:9
  126.0 16.4 %all-to-all-start.3 = ((f32[16,1,4096]{2,1,0:T(1,128)}), f32[16,1,4096]{2,1,0:T(1,128)S(1)}, u32[]{:S(2)}, u32[]{:S(2)}) async-start(f32[16,1,4096]{2,1,0:T(1,128)} %reshape.1650), calls=%async_computation.3 | async-start | bytes 524288 | tf_op jit(solution)/shard_map/all_to_all | solution.py:13
  144.5 75.1 %all-to-all-start.4 = ((bf16[16,2,3,32,512]{4,3,2,1,0:T(8,128)(2,1)}), bf16[16,2,3,32,512]{4,3,2,1,0:T(8,128)(2,1)}, u32[]{:S(2)}, u32[]{:S(2)}) async-start(bf16[16,2,3,32,512]{4,3,2,1,0:T(8,128)(2,1)} %stack.24), calls=%async_computation.4 | async-start | bytes 6291456 | tf_op jit(solution)/shard_map/all_to_all | solution.py:63
  156.6 4.7 copy-start.17
  156.6 4.8 copy-start.18
  156.7 4.8 copy-start.19
  159.5 31.6 %collective-permute-start.2 = (f32[2,3,3,32,512]{4,3,2,1,0:T(8,128)S(1)}, f32[2,3,3,32,512]{4,3,2,1,0:T(8,128)}, u32[]{:S(2)}, u32[]{:S(2)}) collective-permute-start(f32[2,3,3,32,512]{4,3,2,1,0:T(8,128)S(1)} %maximum_maximum_fusion.2), channel_id=1, source_target_pairs={{0,16},{16,32},{32,48},{48,64},{64,80},{80,96},{96,112},{112,128},... | collective-permute-start | bytes 3538952 | tf_op jit(solution)/shard_map/ppermute | solution.py:9
  219.5 2.2 copy-start.1
  231.2 20.1 %all-to-all-start.5 = ((f32[16,1,6144]{2,1,0:T(1,128)}), f32[16,1,6144]{2,1,0:T(1,128)}, u32[]{:S(2)}, u32[]{:S(2)}) async-start(f32[16,1,6144]{2,1,0:T(1,128)} %reshape.1652), calls=%async_computation.5 | async-start | bytes 786432 | tf_op jit(solution)/shard_map/all_to_all | solution.py:13
  253.8 97.2 %all-to-all-start.6 = ((bf16[16,2,4,32,512]{4,3,2,1,0:T(8,128)(2,1)}), bf16[16,2,4,32,512]{4,3,2,1,0:T(8,128)(2,1)}, u32[]{:S(2)}, u32[]{:S(2)}) async-start(bf16[16,2,4,32,512]{4,3,2,1,0:T(8,128)(2,1)} %stack.25), calls=%async_computation.6 | async-start | bytes 8388608 | tf_op jit(solution)/shard_map/all_to_all | solution.py:63
  271.6 3.4 copy-start.2
  271.6 3.4 copy-start.5
  271.6 3.4 copy-start.7
  275.3 80.7 %collective-permute-start.3 = (f32[2,4,4,32,512]{4,3,2,1,0:T(8,128)S(1)}, f32[2,4,4,32,512]{4,3,2,1,0:T(8,128)}, u32[]{:S(2)}, u32[]{:S(2)}) collective-permute-start(f32[2,4,4,32,512]{4,3,2,1,0:T(8,128)S(1)} %maximum_maximum_fusion.1), channel_id=1, source_target_pairs={{0,16},{16,32},{32,48},{48,64},{64,80},{80,96},{96,112},{112,128},... | collective-permute-start | bytes 6291464 | tf_op jit(solution)/shard_map/ppermute | solution.py:9
  351.0 5.0 copy-start.3
  351.0 5.0 copy-start.6
  351.0 5.0 copy-start.8
  364.4 2.8 copy-start.4
  375.2 22.7 %all-to-all-start.7 = ((f32[16,1,8192]{2,1,0:T(1,128)}), f32[16,1,8192]{2,1,0:T(1,128)S(1)}, u32[]{:S(2)}, u32[]{:S(2)}) async-start(f32[16,1,8192]{2,1,0:T(1,128)} %reshape.1654), calls=%async_computation.7 | async-start | bytes 1048576 | tf_op jit(solution)/shard_map/all_to_all | solution.py:13
  397.9 3.0 copy-start.9
  401.0 119.4 %all-to-all-start.8 = ((bf16[16,2,5,32,512]{4,3,2,1,0:T(8,128)(2,1)}), bf16[16,2,5,32,512]{4,3,2,1,0:T(8,128)(2,1)}, u32[]{:S(2)}, u32[]{:S(2)}) async-start(bf16[16,2,5,32,512]{4,3,2,1,0:T(8,128)(2,1)} %stack.26), calls=%async_computation.8 | async-start | bytes 10485760 | tf_op jit(solution)/shard_map/all_to_all | solution.py:63
  415.3 2.3 copy-start.12
  415.3 2.3 copy-start.13
  424.6 101.4 %collective-permute-start.4 = (f32[2,5,5,32,512]{4,3,2,1,0:T(8,128)}, f32[2,5,5,32,512]{4,3,2,1,0:T(8,128)}, u32[]{:S(2)}, u32[]{:S(2)}) collective-permute-start(f32[2,5,5,32,512]{4,3,2,1,0:T(8,128)} %maximum_maximum_fusion), channel_id=1, source_target_pairs={{0,16},{16,32},{32,48},{48,64},{64,80},{80,96},{96,112},{112,128},... | collective-permute-start | bytes 9830408 | tf_op jit(solution)/shard_map/ppermute | solution.py:9
  549.8 25.6 %all-to-all-start.9 = ((f32[16,1,10240]{2,1,0:T(1,128)}), f32[16,1,10240]{2,1,0:T(1,128)S(1)}, u32[]{:S(2)}, u32[]{:S(2)}) async-start(f32[16,1,10240]{2,1,0:T(1,128)} %reshape.1656), calls=%async_computation.9 | async-start | bytes 1310720 | tf_op jit(solution)/shard_map/all_to_all | solution.py:13
  584.9 2.5 copy-start.14
  584.9 2.5 copy-start.15
